TPU v7x, 32 devices: a whole 2x2x4 slice. The times are simulated.
32 devices in a mesh: wide: 8 (over y, x, core), narrow: 4 (over z).
Axes of the slice: x: 2, y: 2, z: 4, core: 2. Of those that a mesh axis runs over, the one named last changes fastest.
Arguments:
- tokens: bfloat16 [16, 1024, 768], P('wide', 'narrow'), may hold values from -6 to 6
- step_ids: int32 [16], P('wide'), may hold values from 0 to 999
- prefix: int32 [16], P('wide'), may hold values from 1 to 1024, as said below
- keep_bits: int32 [16, 1024], P('wide'), may hold values 0 or 1
- ada_weight: bfloat16 [4608, 128], replicated, may hold values from -0.5 to 0.5
- ada_bias: float32 [4608], replicated, may hold values from -3 to 3
- norm1_gain: float32 [768], replicated, may hold values from 0.5 to 1.5
- qkv_weight: bfloat16 [768, 2304], replicated, may hold values from -0.21875 to 0.21875
- out_weight: bfloat16 [768, 768], replicated, may hold values from -6 to 6
- norm2_gain: float32 [768], replicated, may hold values from 0.5 to 1.5
- up_weight: bfloat16 [768, 3072], replicated, may hold values from -0.21875 to 0.21875
- up_bias: float32 [3072], replicated, may hold values from -3 to 3
- down_weight: bfloat16 [3072, 768], replicated, may hold values from -0.21875 to 0.21875
- down_bias: float32 [768], replicated, may hold values from -3 to 3
- cotangent: bfloat16 [16, 1024, 768], P('wide', 'narrow'), may hold values from -6 to 6
Outputs:
- out_tokens: bfloat16 [16, 1024, 768], P('wide', 'narrow')
- input_grad: bfloat16 [16, 1024, 768], P('wide', 'narrow')
- ada_weight_grad: float32 [4608, 128], replicated
- ada_bias_grad: float32 [4608], replicated
- norm1_gain_grad: float32 [768], replicated
- qkv_weight_grad: float32 [768, 2304], replicated
- out_weight_grad: float32 [768, 768], replicated
- norm2_gain_grad: float32 [768], replicated
- up_weight_grad: float32 [768, 3072], replicated
- up_bias_grad: float32 [3072], replicated
- down_weight_grad: float32 [3072, 768], replicated
- down_bias_grad: float32 [768], replicated
Inputs may be any that keep to these rules, and one draw needn't show every extreme that they name: Every prefix keeps at least the first position visible; of the 2 consecutive sequences of each index of wide, one has the whole length 1024 as prefix.
All inputs are finite; a program needn't handle non-finite values. No bound on the sum of `keep_bits` on one device may be relied on, other than what follows from the above.
Results may differ from a plain program's by a relative error of at most 0.015.
Values may be sent and summed in bfloat16 or wider, within the bound.
A program may use at most 192 MiB of HBM per device.

v0:
```python
import functools
import math
import jax
import jax.numpy as jnp
from jax import lax
from jax.sharding import PartitionSpec as P

HEAD = 64
TEMB = 128
MICRO = 2
norm_epsilon = 1e-05
gelu_coeff = 0.7978845608028654
masked_score = -1e30


def shifted(block, axis, distance):
    devices = range(lax.axis_size(axis))
    route = [((i - distance) % len(devices), i) for i in devices]
    return lax.ppermute(block, axis, route)


def time_embed(step_ids):
    halfway = TEMB // 2
    frequency = jnp.exp(jnp.arange(halfway, dtype=jnp.float32) * (-math.log(10000.0) / halfway))
    angles = step_ids.astype(jnp.float32)[:, None] * frequency[None, :]
    return jnp.concatenate([jnp.cos(angles), jnp.sin(angles)], axis=-1)


def rope_tables(positions):
    halfway = HEAD // 2
    inverse = jnp.exp(jnp.arange(halfway, dtype=jnp.float32) * (-2.0 * math.log(10000.0) / HEAD))
    angles = positions[:, None] * inverse[None, :]
    return (jnp.cos(angles), jnp.sin(angles))


def rotate(values, cosine_rows, sine_rows):
    halfway = values.shape[-1] // 2
    former = values[..., :halfway]
    latter = values[..., halfway:]
    cos_wide = cosine_rows[:, None, :]
    sin_wide = sine_rows[:, None, :]
    return jnp.concatenate(
        [former * cos_wide - latter * sin_wide, latter * cos_wide + former * sin_wide], axis=-1
    )


def rotate_back(incoming, cosine_rows, sine_rows):
    halfway = incoming.shape[-1] // 2
    former = incoming[..., :halfway]
    latter = incoming[..., halfway:]
    cos_wide = cosine_rows[:, None, :]
    sin_wide = sine_rows[:, None, :]
    return jnp.concatenate(
        [former * cos_wide + latter * sin_wide, latter * cos_wide - former * sin_wide], axis=-1
    )


def layer_norm(values, scaling):
    center = values - jnp.mean(values, axis=-1, keepdims=True)
    spread = jnp.mean(center * center, axis=-1, keepdims=True)
    return center * lax.rsqrt(spread + norm_epsilon) * scaling


def modulate(values, scaling, shift_rows, scale_rows):
    return layer_norm(values, scaling) * (1.0 + scale_rows) + shift_rows


def gelu_tanh(values):
    inner_arg = gelu_coeff * (values + 0.044715 * values * values * values)
    return 0.5 * values * (1.0 + jnp.tanh(inner_arg))


def pass_pairs(pair_block):
    return shifted(pair_block, "narrow", 1)


def pass_pairs_again(pair_block):
    return shifted(pair_block, "narrow", 1)


def pass_grads(grad_block):
    return shifted(grad_block.astype(jnp.bfloat16), "narrow", 1).astype(grad_block.dtype)


def add_trees(former_tree, latter_tree):
    return jax.tree.map(jnp.add, former_tree, latter_tree)


def local(
    tokens,
    step_ids,
    prefix,
    keep_bits,
    ada_weight,
    ada_bias,
    norm1_gain,
    qkv_weight,
    out_weight,
    norm2_gain,
    up_weight,
    up_bias,
    down_weight,
    down_bias,
    cotangent,
):
    cycle_size = lax.axis_size("narrow")
    cycle_index = lax.axis_index("narrow")
    groups, span_size, width = tokens.shape
    per_micro = groups // MICRO
    head_count = width // HEAD
    score_scale = HEAD ** (-0.5)
    offsets = jnp.arange(span_size, dtype=jnp.int32)
    cosine_rows, sine_rows = rope_tables((cycle_index * span_size + offsets).astype(jnp.float32))
    condition = jax.nn.silu(time_embed(step_ids))
    modulation = (
        jnp.dot(
            condition,
            ada_weight.astype(jnp.float32).T,
            precision=lax.Precision.HIGHEST,
            preferred_element_type=jnp.float32,
        )
        + ada_bias
    )
    last_source = (cycle_index + 1) % cycle_size
    outputs = []
    input_grads = []
    collected = []
    for micro_index in range(MICRO):
        picked = slice(micro_index * per_micro, (micro_index + 1) * per_micro)
        inputs = tokens[picked].astype(jnp.float32)
        leading = prefix[picked]
        bits_here = keep_bits[picked]
        shift_one, scale_one, gate_one, shift_two, scale_two, gate_two = jnp.split(
            modulation[picked][:, None, :], 6, axis=-1
        )
        normed, norm_back = jax.vjp(modulate, inputs, norm1_gain, shift_one, scale_one)
        normed_low = normed.astype(jnp.bfloat16)
        projected = jnp.einsum(
            "bcd,de->bce", normed_low, qkv_weight, preferred_element_type=jnp.float32
        )
        shaped = projected.reshape(per_micro, span_size, 3, head_count, HEAD)
        queries = rotate(shaped[:, :, 0], cosine_rows, sine_rows).astype(jnp.bfloat16)
        key_rows = (
            rotate(shaped[:, :, 1], cosine_rows, sine_rows)
            .astype(jnp.bfloat16)
            .reshape(per_micro, span_size, width)
        )
        value_rows = shaped[:, :, 2].astype(jnp.bfloat16).reshape(per_micro, span_size, width)
        pair_rows = jnp.stack([key_rows, value_rows])

        def visible_keys(source):
            first_key = source * span_size
            window = lax.dynamic_slice_in_dim(bits_here, first_key, span_size, 1)
            allowed = ((first_key + offsets)[None, :] < leading[:, None]) | (window == 1)
            return allowed[:, None, None, :]

        def key_scores(key_block):
            shaped_keys = key_block.reshape(per_micro, span_size, head_count, HEAD)
            return (
                jnp.einsum(
                    "bqhe,bkhe->bhqk", queries, shaped_keys, preferred_element_type=jnp.float32
                )
                * score_scale
            )

        def add_online(pair_block, source, running):
            highest, total_sum, summed = running
            scores = key_scores(pair_block[0])
            allowed = visible_keys(source)
            block_high = jnp.max(jnp.where(allowed, scores, masked_score), axis=-1)
            new_high = jnp.maximum(highest, block_high)
            factor = jnp.exp(highest - new_high)
            exp_terms = jnp.where(allowed, jnp.exp(scores - new_high[..., None]), 0.0)
            total_sum = total_sum * factor + jnp.sum(exp_terms, axis=-1)
            shaped_values = pair_block[1].reshape(per_micro, span_size, head_count, HEAD)
            summed = summed * jnp.transpose(factor, (0, 2, 1))[..., None] + jnp.einsum(
                "bhqk,bkhe->bqhe",
                exp_terms.astype(jnp.bfloat16),
                shaped_values,
                preferred_element_type=jnp.float32,
            )
            return (new_high, total_sum, summed)

        start_stats = (
            jnp.full((per_micro, head_count, span_size), masked_score, jnp.float32),
            jnp.zeros((per_micro, head_count, span_size), jnp.float32),
        )
        start_sum = jnp.zeros((per_micro, span_size, head_count, HEAD), jnp.float32)

        def online_turn(turn_index, carried):
            pair_block, running = carried
            running = add_online(pair_block, (cycle_index - turn_index) % cycle_size, running)
            return (pass_pairs(pair_block), running)

        pair_block, running = lax.fori_loop(
            0, cycle_size - 1, online_turn, (pair_rows, (start_stats[0], start_stats[1], start_sum))
        )
        highest, total_sum, summed = add_online(pair_block, last_source, running)
        attended = summed / jnp.transpose(total_sum, (0, 2, 1))[..., None]
        log_total = highest + jnp.log(total_sum)
        attended_low = attended.reshape(per_micro, span_size, width).astype(jnp.bfloat16)
        branch_one = jnp.einsum(
            "bcd,de->bce", attended_low, out_weight, preferred_element_type=jnp.float32
        )
        middle = inputs + gate_one * branch_one
        normed_two, norm_back_two = jax.vjp(modulate, middle, norm2_gain, shift_two, scale_two)
        normed_two_low = normed_two.astype(jnp.bfloat16)
        hidden = (
            jnp.einsum("bcd,df->bcf", normed_two_low, up_weight, preferred_element_type=jnp.float32)
            + up_bias
        )
        active, gelu_back = jax.vjp(gelu_tanh, hidden)
        active_low = active.astype(jnp.bfloat16)
        branch_two = (
            jnp.einsum("bcf,fd->bcd", active_low, down_weight, preferred_element_type=jnp.float32)
            + down_bias
        )
        outputs.append((middle + gate_two * branch_two).astype(jnp.bfloat16))
        out_grad = cotangent[picked].astype(jnp.float32)
        gate_two_grad = jnp.sum(out_grad * branch_two, axis=1, keepdims=True)
        branch_two_grad = (gate_two * out_grad).astype(jnp.bfloat16)
        down_grad = jnp.einsum(
            "bcf,bcd->fd", active_low, branch_two_grad, preferred_element_type=jnp.float32
        )
        down_bias_grad = jnp.sum(branch_two_grad.astype(jnp.float32), axis=(0, 1))
        (hidden_grad,) = gelu_back(
            jnp.einsum(
                "bcd,fd->bcf", branch_two_grad, down_weight, preferred_element_type=jnp.float32
            )
        )
        hidden_low = hidden_grad.astype(jnp.bfloat16)
        up_grad = jnp.einsum(
            "bcd,bcf->df", normed_two_low, hidden_low, preferred_element_type=jnp.float32
        )
        up_bias_grad = jnp.sum(hidden_low.astype(jnp.float32), axis=(0, 1))
        middle_part, gain_two_grad, shift_two_grad, scale_two_grad = norm_back_two(
            jnp.einsum("bcf,df->bcd", hidden_low, up_weight, preferred_element_type=jnp.float32)
        )
        middle_grad = out_grad + middle_part
        gate_one_grad = jnp.sum(middle_grad * branch_one, axis=1, keepdims=True)
        branch_one_grad = (gate_one * middle_grad).astype(jnp.bfloat16)
        out_weight_part = jnp.einsum(
            "bcd,bce->de", attended_low, branch_one_grad, preferred_element_type=jnp.float32
        )
        attended_grad = (
            jnp.einsum(
                "bce,de->bcd", branch_one_grad, out_weight, preferred_element_type=jnp.float32
            )
            .astype(jnp.bfloat16)
            .reshape(per_micro, span_size, head_count, HEAD)
        )
        row_delta = jnp.einsum("bqhe,bqhe->bhq", attended_grad.astype(jnp.float32), attended)

        def add_grads(pair_block, source, query_grad):
            scores = key_scores(pair_block[0])
            prob_rows = jnp.where(visible_keys(source), jnp.exp(scores - log_total[..., None]), 0.0)
            shaped_keys = pair_block[0].reshape(per_micro, span_size, head_count, HEAD)
            shaped_values = pair_block[1].reshape(per_micro, span_size, head_count, HEAD)
            value_part = jnp.einsum(
                "bhqk,bqhe->bkhe",
                prob_rows.astype(jnp.bfloat16),
                attended_grad,
                preferred_element_type=jnp.float32,
            )
            prob_grad = jnp.einsum(
                "bqhe,bkhe->bhqk", attended_grad, shaped_values, preferred_element_type=jnp.float32
            )
            score_grad = (prob_rows * (prob_grad - row_delta[..., None])).astype(jnp.bfloat16)
            query_grad = (
                query_grad
                + jnp.einsum(
                    "bhqk,bkhe->bqhe", score_grad, shaped_keys, preferred_element_type=jnp.float32
                )
                * score_scale
            )
            key_part = (
                jnp.einsum(
                    "bhqk,bqhe->bkhe", score_grad, queries, preferred_element_type=jnp.float32
                )
                * score_scale
            )
            return (
                query_grad,
                jnp.stack(
                    [
                        key_part.reshape(per_micro, span_size, width),
                        value_part.reshape(per_micro, span_size, width),
                    ]
                ),
            )

        start_query = jnp.zeros((per_micro, span_size, head_count, HEAD), jnp.float32)

        def grads_turn(turn_index, carried):
            pair_block, grad_block, query_grad = carried
            query_grad, key_value_part = add_grads(
                pair_block, (cycle_index - turn_index) % cycle_size, query_grad
            )
            return (
                pass_pairs_again(pair_block),
                pass_grads(grad_block + key_value_part),
                query_grad,
            )

        start_grads = jnp.zeros((2, per_micro, span_size, width), jnp.float32)
        pair_block, grad_block, query_grad = lax.fori_loop(
            0, cycle_size - 1, grads_turn, (pair_rows, start_grads, start_query)
        )
        query_grad, key_value_part = add_grads(pair_block, last_source, query_grad)
        pair_grads = pass_grads(grad_block + key_value_part)
        query_pre = rotate_back(query_grad, cosine_rows, sine_rows).reshape(
            per_micro, span_size, width
        )
        key_pre = rotate_back(
            pair_grads[0].reshape(per_micro, span_size, head_count, HEAD), cosine_rows, sine_rows
        ).reshape(per_micro, span_size, width)
        joined = jnp.concatenate([query_pre, key_pre, pair_grads[1]], axis=-1).astype(jnp.bfloat16)
        qkv_grad = jnp.einsum("bcd,bce->de", normed_low, joined, preferred_element_type=jnp.float32)
        input_part, gain_one_grad, shift_one_grad, scale_one_grad = norm_back(
            jnp.einsum("bce,de->bcd", joined, qkv_weight, preferred_element_type=jnp.float32)
        )
        input_grads.append((middle_grad + input_part).astype(jnp.bfloat16))
        mod_grad = jnp.concatenate(
            [
                shift_one_grad,
                scale_one_grad,
                gate_one_grad,
                shift_two_grad,
                scale_two_grad,
                gate_two_grad,
            ],
            axis=-1,
        )[:, 0, :]
        ada_grad = jnp.dot(
            mod_grad.T,
            condition[picked],
            precision=lax.Precision.HIGHEST,
            preferred_element_type=jnp.float32,
        )
        ada_bias_grad = jnp.sum(mod_grad, axis=0)
        collected.append(
            (
                ada_grad,
                ada_bias_grad,
                gain_one_grad,
                qkv_grad,
                out_weight_part,
                gain_two_grad,
                up_grad,
                up_bias_grad,
                down_grad,
                down_bias_grad,
            )
        )
    summed = functools.reduce(add_trees, collected)
    finals = lax.psum(
        (
            summed[0],
            summed[1],
            summed[2],
            summed[3],
            summed[4],
            summed[5],
            summed[6],
            summed[7],
            summed[8],
            summed[9],
        ),
        ("wide", "narrow"),
    )
    return (
        jnp.concatenate(outputs, axis=0),
        jnp.concatenate(input_grads, axis=0),
        finals[0],
        finals[1],
        finals[2],
        finals[3],
        finals[4],
        finals[5],
        finals[6],
        finals[7],
        finals[8],
        finals[9],
    )


def solution(mesh):
    in_specs = (
        P("wide", "narrow", None),
        P("wide"),
        P("wide"),
        P("wide", None),
        P(),
        P(),
        P(),
        P(),
        P(),
        P(),
        P(),
        P(),
        P(),
        P(),
        P("wide", "narrow", None),
    )
    out_specs = (
        P("wide", "narrow", None),
        P("wide", "narrow", None),
        P(),
        P(),
        P(),
        P(),
        P(),
        P(),
        P(),
        P(),
        P(),
        P(),
    )
    return jax.shard_map(local, mesh=mesh, in_specs=in_specs, out_specs=out_specs, check_vma=False)
```

profile of v0, /device:TPU:0, one launch (start us, length us, event | category | flops | bytes accessed | tf_op | source)
XLA Modules:
  0.0 1062.0 jit_solution(13036474322672682413)
XLA Ops:
  14.5 5.8 copy.51
  39.6 66.5 %while.85 = (s32[]{:T(128)}, bf16[2,1,256,768]{2,3,1,0:T(8,128)(2,1)}, f32[1,12,256]{2,1,0:T(8,128)}, f32[1,12,256]{2,1,0:T(8,128)}, f32[1,256,12,64]{1,3,2,0:T(...) while((s32[]{:T(128)}, ...), condition=%wide.region_15.16_spmd.clone, body=%wide.region_12.15_spmd.clone.sunk | while | flops 210586640 | bytes 25119744 | solution.py:195
  48.7 14.7 %collective-permute-done.1 = bf16[2,1,256,768]{2,3,1,0:T(8,128)(2,1)} collective-permute-done((bf16[2,1,256,768]{2,3,1,0:T(8,128)(2,1)S(1)}, bf16[2,1,256,768]{2,3,1,0:T(8,128)(2,1)}, u32[]{:S(2)}, u32[]{:S(2)}) %collective-permute-start.1) | collective-permute-done | bytes 786464 | tf_op jit(solution)/shard_map/while/body/eval_jaxpr/ppermute | solution.py:19
  69.5 15.7 %collective-permute-done.1 = bf16[2,1,256,768]{2,3,1,0:T(8,128)(2,1)} collective-permute-done((bf16[2,1,256,768]{2,3,1,0:T(8,128)(2,1)S(1)}, bf16[2,1,256,768]{2,3,1,0:T(8,128)(2,1)}, u32[]{:S(2)}, u32[]{:S(2)}) %collective-permute-start.1) | collective-permute-done | bytes 786464 | tf_op jit(solution)/shard_map/while/body/eval_jaxpr/ppermute | solution.py:19
  91.3 14.8 %collective-permute-done.1 = bf16[2,1,256,768]{2,3,1,0:T(8,128)(2,1)} collective-permute-done((bf16[2,1,256,768]{2,3,1,0:T(8,128)(2,1)S(1)}, bf16[2,1,256,768]{2,3,1,0:T(8,128)(2,1)}, u32[]{:S(2)}, u32[]{:S(2)}) %collective-permute-start.1) | collective-permute-done | bytes 786464 | tf_op jit(solution)/shard_map/while/body/eval_jaxpr/ppermute | solution.py:19
  108.2 57.2 %while.84 = (s32[]{:T(128)}, bf16[2,1,256,768]{2,3,1,0:T(8,128)(2,1)}, f32[1,12,256]{2,1,0:T(8,128)S(1)}, f32[1,12,256]{2,1,0:T(8,128)}, f32[1,256,12,64]{1,3,2,...) while((s32[]{:T(128)}, ...), condition=%wide.region_5.6_spmd.clone, body=%wide.region_2.5_spmd.clone.sunk | while | flops 210586640 | bytes 25070564 | solution.py:195
  113.6 14.5 %collective-permute-done = bf16[2,1,256,768]{2,3,1,0:T(8,128)(2,1)} collective-permute-done((bf16[2,1,256,768]{2,3,1,0:T(8,128)(2,1)S(1)}, bf16[2,1,256,768]{2,3,1,0:T(8,128)(2,1)}, u32[]{:S(2)}, u32[]{:S(2)}) %collective-permute-start) | collective-permute-done | bytes 786464 | tf_op jit(solution)/shard_map/while/body/eval_jaxpr/ppermute | solution.py:19
  133.5 13.6 %collective-permute-done = bf16[2,1,256,768]{2,3,1,0:T(8,128)(2,1)} collective-permute-done((bf16[2,1,256,768]{2,3,1,0:T(8,128)(2,1)S(1)}, bf16[2,1,256,768]{2,3,1,0:T(8,128)(2,1)}, u32[]{:S(2)}, u32[]{:S(2)}) %collective-permute-start) | collective-permute-done | bytes 786464 | tf_op jit(solution)/shard_map/while/body/eval_jaxpr/ppermute | solution.py:19
  152.5 12.7 %collective-permute-done = bf16[2,1,256,768]{2,3,1,0:T(8,128)(2,1)} collective-permute-done((bf16[2,1,256,768]{2,3,1,0:T(8,128)(2,1)S(1)}, bf16[2,1,256,768]{2,3,1,0:T(8,128)(2,1)}, u32[]{:S(2)}, u32[]{:S(2)}) %collective-permute-start) | collective-permute-done | bytes 786464 | tf_op jit(solution)/shard_map/while/body/eval_jaxpr/ppermute | solution.py:19
  202.8 131.9 %while.86 = (s32[]{:T(128)}, bf16[2,1,256,768]{2,3,1,0:T(8,128)(2,1)}, f32[2,1,256,768]{2,3,1,0:T(8,128)}, f32[1,256,12,64]{1,3,2,0:T(8,128)}, s32[]{:T(128)}, /...) while((s32[]{:T(128)}, ...), condition=%wide.region_23.24_spmd.clone, body=%wide.region_22.23_spmd.clone.sunk | while | flops 513934336 | bytes 45259516 | solution.py:306
  217.1 20.1 %collective-permute-done.3 = bf16[2,1,256,768]{2,3,1,0:T(8,128)(2,1)} collective-permute-done((bf16[2,1,256,768]{2,3,1,0:T(8,128)(2,1)}, bf16[2,1,256,768]{2,3,1,0:T(8,128)(2,1)}, u32[]{:S(2)}, u32[]{:S(2)}) %collective-permute-start.3) | collective-permute-done | bytes 786464 | tf_op jit(solution)/shard_map/while/body/eval_jaxpr/ppermute | solution.py:19
  239.5 8.1 collective-permute-done.2
  262.3 19.8 %collective-permute-done.3 = bf16[2,1,256,768]{2,3,1,0:T(8,128)(2,1)} collective-permute-done((bf16[2,1,256,768]{2,3,1,0:T(8,128)(2,1)}, bf16[2,1,256,768]{2,3,1,0:T(8,128)(2,1)}, u32[]{:S(2)}, u32[]{:S(2)}) %collective-permute-start.3) | collective-permute-done | bytes 786464 | tf_op jit(solution)/shard_map/while/body/eval_jaxpr/ppermute | solution.py:19
  284.5 7.2 collective-permute-done.2
  306.2 19.8 %collective-permute-done.3 = bf16[2,1,256,768]{2,3,1,0:T(8,128)(2,1)} collective-permute-done((bf16[2,1,256,768]{2,3,1,0:T(8,128)(2,1)}, bf16[2,1,256,768]{2,3,1,0:T(8,128)(2,1)}, u32[]{:S(2)}, u32[]{:S(2)}) %collective-permute-start.3) | collective-permute-done | bytes 786464 | tf_op jit(solution)/shard_map/while/body/eval_jaxpr/ppermute | solution.py:19
  328.4 6.2 collective-permute-done.2
  348.8 126.2 %while.87 = (s32[]{:T(128)}, bf16[2,1,256,768]{2,3,1,0:T(8,128)(2,1)}, f32[2,1,256,768]{2,3,1,0:T(8,128)}, f32[1,256,12,64]{1,3,2,0:T(8,128)}, s32[]{:T(128)}, /...) while((s32[]{:T(128)}, ...), condition=%wide.region_29.30_spmd.clone, body=%wide.region_28.29_spmd.clone.sunk | while | flops 513934336 | bytes 42212092 | solution.py:306
  360.1 20.4 %collective-permute-done.5 = bf16[2,1,256,768]{2,3,1,0:T(8,128)(2,1)} collective-permute-done((bf16[2,1,256,768]{2,3,1,0:T(8,128)(2,1)}, bf16[2,1,256,768]{2,3,1,0:T(8,128)(2,1)}, u32[]{:S(2)}, u32[]{:S(2)}) %collective-permute-start.5) | collective-permute-done | bytes 786464 | tf_op jit(solution)/shard_map/while/body/eval_jaxpr/ppermute | solution.py:19
  383.0 9.0 collective-permute-done.4
  403.6 19.9 %collective-permute-done.5 = bf16[2,1,256,768]{2,3,1,0:T(8,128)(2,1)} collective-permute-done((bf16[2,1,256,768]{2,3,1,0:T(8,128)(2,1)}, bf16[2,1,256,768]{2,3,1,0:T(8,128)(2,1)}, u32[]{:S(2)}, u32[]{:S(2)}) %collective-permute-start.5) | collective-permute-done | bytes 786464 | tf_op jit(solution)/shard_map/while/body/eval_jaxpr/ppermute | solution.py:19
  425.9 8.0 collective-permute-done.4
  445.5 19.9 %collective-permute-done.5 = bf16[2,1,256,768]{2,3,1,0:T(8,128)(2,1)} collective-permute-done((bf16[2,1,256,768]{2,3,1,0:T(8,128)(2,1)}, bf16[2,1,256,768]{2,3,1,0:T(8,128)(2,1)}, u32[]{:S(2)}, u32[]{:S(2)}) %collective-permute-start.5) | collective-permute-done | bytes 786464 | tf_op jit(solution)/shard_map/while/body/eval_jaxpr/ppermute | solution.py:19
  467.8 7.1 collective-permute-done.4
  493.5 5.4 convolution_add_fusion.7
  500.1 5.3 convolution_add_fusion.1
  505.5 6.9 convolution_add_fusion.2
  512.5 6.3 convert_reduce_fusion.4
  554.5 7.9 convolution_add_fusion
  573.2 42.2 %all-reduce = (f32[4608]{0:T(1024)}, f32[768]{0:T(1024)}, f32[768]{0:T(1024)}, f32[3072]{0:T(1024)}, f32[768]{0:T(1024)}) all-reduce(f32[4608]{0:T(1024)S(1)} %add.737, f32[768]{0:T(1024)S(1)} %add.738, f32[768]{0:T(1024)} %add.741, f32[3072]{0:T(1024)} %add.743, f32[768]{0:T(1024)} %add.745), channel_id=1, replica_groups=mesh['wide'=8,'narrow'=4] {'wide','narrow'}, use_global_device_ids=true, to_apply=%region_45.46 | all-reduce | flops 9984 | bytes 79872 | tf_op jit(solution)/shard_map/psum | solution.py:356
  620.4 410.0 %all-reduce.4.cloned.1.call-done = (f32[4608,128]{1,0:T(8,128)}, f32[768,2304]{1,0:T(8,128)}, f32[768,768]{1,0:T(8,128)}, f32[768,3072]{1,0:T(8,128)}, f32[3072,768]{1,0:T(8,128)}) async-done(((f32[4608,128]{1,0:T(8,128)}, f32[768,2304]{1,0:T(8,128)}, f32[768,768]{1,0:T(8,128)}, f32[768,3072]{1,0:T(8,128)}, f32[3072,768]{1,0:T(8,128)}), (f32[4608,128]{1,0:T(8,128)}, f32[768,2304]{1,0:T(8,128)}, ...) | async-done | bytes 30670864 | tf_op jit(solution)/shard_map/psum | solution.py:356
  1033.7 6.6 copy.172
  1041.7 9.3 copy.174
  (685 shorter events, 287.0 us)
Async XLA Ops:
  7.2 168.4 %copy-start = (bf16[768,768]{1,0:T(8,128)(2,1)S(1)}, bf16[768,768]{1,0:T(8,128)(2,1)}, u32[]{:S(2)}) copy-start(bf16[768,768]{1,0:T(8,128)(2,1)} %param.31) | copy-start | bytes 3538948
  7.2 1023.2 %all-reduce.4.cloned.1.call-start = ((), (), s32[]{:S(2)}) async-start(), calls=%async_computation | async-start | bytes 61341696 | tf_op jit(solution)/shard_map/psum | solution.py:356
  33.4 74.8 %copy-start.47 = (bf16[1,256,12,32]{1,3,2,0:T(8,128)(2,1)}, bf16[1,256,12,32]{1,3,2,0:T(8,128)(2,1)S(1)}, u32[]{:S(2)}) copy-start(bf16[1,256,12,32]{1,3,2,0:T(8,128)(2,1)S(1)} %get-tuple-element.1423) | copy-start | bytes 589828
  33.4 74.8 %copy-start.49 = (bf16[1,256,12,32]{1,3,2,0:T(8,128)(2,1)}, bf16[1,256,12,32]{1,3,2,0:T(8,128)(2,1)S(1)}, u32[]{:S(2)}) copy-start(bf16[1,256,12,32]{1,3,2,0:T(8,128)(2,1)S(1)} %get-tuple-element.1424) | copy-start | bytes 589828
  40.8 22.7 %collective-permute-start.1 = (bf16[2,1,256,768]{2,3,1,0:T(8,128)(2,1)S(1)}, bf16[2,1,256,768]{2,3,1,0:T(8,128)(2,1)}, u32[]{:S(2)}, u32[]{:S(2)}) collective-permute-start(bf16[2,1,256,768]{2,3,1,0:T(8,128)(2,1)S(1)} %copy.108), channel_id=1, source_target_pairs={{3,0},{0,1},{1,2},{2,3},{7,4},{4,5},{5,6},{6,7},{11,8},{8,9},{9,10... | collective-permute-start | bytes 2359304 | tf_op jit(solution)/shard_map/while/body/eval_jaxpr/ppermute | solution.py:19
  64.6 20.6 %collective-permute-start.1 = (bf16[2,1,256,768]{2,3,1,0:T(8,128)(2,1)S(1)}, bf16[2,1,256,768]{2,3,1,0:T(8,128)(2,1)}, u32[]{:S(2)}, u32[]{:S(2)}) collective-permute-start(bf16[2,1,256,768]{2,3,1,0:T(8,128)(2,1)S(1)} %copy.108), channel_id=1, source_target_pairs={{3,0},{0,1},{1,2},{2,3},{7,4},{4,5},{5,6},{6,7},{11,8},{8,9},{9,10... | collective-permute-start | bytes 2359304 | tf_op jit(solution)/shard_map/while/body/eval_jaxpr/ppermute | solution.py:19
  68.1 17.2 %copy-start.83 = (f32[1,12,256]{2,1,0:T(8,128)}, f32[1,12,256]{2,1,0:T(8,128)S(1)}, u32[]{:S(2)}) copy-start(f32[1,12,256]{2,1,0:T(8,128)S(1)} %bitcast_add_fusion.9) | copy-start | bytes 36868 | tf_op jit(solution)/shard_map/while
  86.4 19.7 %collective-permute-start.1 = (bf16[2,1,256,768]{2,3,1,0:T(8,128)(2,1)S(1)}, bf16[2,1,256,768]{2,3,1,0:T(8,128)(2,1)}, u32[]{:S(2)}, u32[]{:S(2)}) collective-permute-start(bf16[2,1,256,768]{2,3,1,0:T(8,128)(2,1)S(1)} %copy.108), channel_id=1, source_target_pairs={{3,0},{0,1},{1,2},{2,3},{7,4},{4,5},{5,6},{6,7},{11,8},{8,9},{9,10... | collective-permute-start | bytes 2359304 | tf_op jit(solution)/shard_map/while/body/eval_jaxpr/ppermute | solution.py:19
  109.3 18.8 %collective-permute-start = (bf16[2,1,256,768]{2,3,1,0:T(8,128)(2,1)S(1)}, bf16[2,1,256,768]{2,3,1,0:T(8,128)(2,1)}, u32[]{:S(2)}, u32[]{:S(2)}) collective-permute-start(bf16[2,1,256,768]{2,3,1,0:T(8,128)(2,1)S(1)} %copy.123), channel_id=1, source_target_pairs={{3,0},{0,1},{1,2},{2,3},{7,4},{4,5},{5,6},{6,7},{11,8},{8,9},{9,10... | collective-permute-start | bytes 2359304 | tf_op jit(solution)/shard_map/while/body/eval_jaxpr/ppermute | solution.py:19
  129.2 17.9 %collective-permute-start = (bf16[2,1,256,768]{2,3,1,0:T(8,128)(2,1)S(1)}, bf16[2,1,256,768]{2,3,1,0:T(8,128)(2,1)}, u32[]{:S(2)}, u32[]{:S(2)}) collective-permute-start(bf16[2,1,256,768]{2,3,1,0:T(8,128)(2,1)S(1)} %copy.123), channel_id=1, source_target_pairs={{3,0},{0,1},{1,2},{2,3},{7,4},{4,5},{5,6},{6,7},{11,8},{8,9},{9,10... | collective-permute-start | bytes 2359304 | tf_op jit(solution)/shard_map/while/body/eval_jaxpr/ppermute | solution.py:19
  148.2 16.9 %collective-permute-start = (bf16[2,1,256,768]{2,3,1,0:T(8,128)(2,1)S(1)}, bf16[2,1,256,768]{2,3,1,0:T(8,128)(2,1)}, u32[]{:S(2)}, u32[]{:S(2)}) collective-permute-start(bf16[2,1,256,768]{2,3,1,0:T(8,128)(2,1)S(1)} %copy.123), channel_id=1, source_target_pairs={{3,0},{0,1},{1,2},{2,3},{7,4},{4,5},{5,6},{6,7},{11,8},{8,9},{9,10... | collective-permute-start | bytes 2359304 | tf_op jit(solution)/shard_map/while/body/eval_jaxpr/ppermute | solution.py:19
  179.1 18.8 %copy-start.23 = (f32[1,256,768]{2,1,0:T(8,128)}, f32[1,256,768]{2,1,0:T(8,128)S(1)}, u32[]{:S(2)}) copy-start(f32[1,256,768]{2,1,0:T(8,128)S(1)} %get-tuple-element.1396) | copy-start | bytes 2359300
  179.1 18.8 %copy-start.118 = (f32[256]{0:T(256)}, f32[256]{0:T(256)S(1)}, u32[]{:S(2)}) copy-start(f32[256]{0:T(256)S(1)} %broadcast_multiply_fusion.2) | copy-start | bytes 3076
  179.6 18.3 %copy-start.134 = (f32[256]{0:T(256)}, f32[256]{0:T(256)S(1)}, u32[]{:S(2)}) copy-start(f32[256]{0:T(256)S(1)} %fusion.244) | copy-start | bytes 3076
  214.5 22.6 %collective-permute-start.3 = (bf16[2,1,256,768]{2,3,1,0:T(8,128)(2,1)}, bf16[2,1,256,768]{2,3,1,0:T(8,128)(2,1)}, u32[]{:S(2)}, u32[]{:S(2)}) collective-permute-start(bf16[2,1,256,768]{2,3,1,0:T(8,128)(2,1)} %fusion.436), channel_id=1, source_target_pairs={{3,0},{0,1},{1,2},{2,3},{7,4},{4,5},{5,6},{6,7},{11,8},{8,9},{9,10... | collective-permute-start | bytes 2359304 | tf_op jit(solution)/shard_map/while/body/eval_jaxpr/ppermute | solution.py:19
  214.5 33.1 %collective-permute-start.2 = (bf16[2,1,256,768]{2,3,1,0:T(8,128)(2,1)}, bf16[2,1,256,768]{2,3,1,0:T(8,128)(2,1)}, u32[]{:S(2)}, u32[]{:S(2)}) collective-permute-start(bf16[2,1,256,768]{2,3,1,0:T(8,128)(2,1)} %copy.149), channel_id=1, source_target_pairs={{3,0},{0,1},{1,2},{2,3},{7,4},{4,5},{5,6},{6,7},{11,8},{8,9},{9,10... | collective-permute-start | bytes 2359304 | tf_op jit(solution)/shard_map/while/body/eval_jaxpr/ppermute | solution.py:19
  259.5 22.6 %collective-permute-start.3 = (bf16[2,1,256,768]{2,3,1,0:T(8,128)(2,1)}, bf16[2,1,256,768]{2,3,1,0:T(8,128)(2,1)}, u32[]{:S(2)}, u32[]{:S(2)}) collective-permute-start(bf16[2,1,256,768]{2,3,1,0:T(8,128)(2,1)} %fusion.436), channel_id=1, source_target_pairs={{3,0},{0,1},{1,2},{2,3},{7,4},{4,5},{5,6},{6,7},{11,8},{8,9},{9,10... | collective-permute-start | bytes 2359304 | tf_op jit(solution)/shard_map/while/body/eval_jaxpr/ppermute | solution.py:19
  259.5 32.2 %collective-permute-start.2 = (bf16[2,1,256,768]{2,3,1,0:T(8,128)(2,1)}, bf16[2,1,256,768]{2,3,1,0:T(8,128)(2,1)}, u32[]{:S(2)}, u32[]{:S(2)}) collective-permute-start(bf16[2,1,256,768]{2,3,1,0:T(8,128)(2,1)} %copy.149), channel_id=1, source_target_pairs={{3,0},{0,1},{1,2},{2,3},{7,4},{4,5},{5,6},{6,7},{11,8},{8,9},{9,10... | collective-permute-start | bytes 2359304 | tf_op jit(solution)/shard_map/while/body/eval_jaxpr/ppermute | solution.py:19
  303.4 22.6 %collective-permute-start.3 = (bf16[2,1,256,768]{2,3,1,0:T(8,128)(2,1)}, bf16[2,1,256,768]{2,3,1,0:T(8,128)(2,1)}, u32[]{:S(2)}, u32[]{:S(2)}) collective-permute-start(bf16[2,1,256,768]{2,3,1,0:T(8,128)(2,1)} %fusion.436), channel_id=1, source_target_pairs={{3,0},{0,1},{1,2},{2,3},{7,4},{4,5},{5,6},{6,7},{11,8},{8,9},{9,10... | collective-permute-start | bytes 2359304 | tf_op jit(solution)/shard_map/while/body/eval_jaxpr/ppermute | solution.py:19
  303.4 31.2 %collective-permute-start.2 = (bf16[2,1,256,768]{2,3,1,0:T(8,128)(2,1)}, bf16[2,1,256,768]{2,3,1,0:T(8,128)(2,1)}, u32[]{:S(2)}, u32[]{:S(2)}) collective-permute-start(bf16[2,1,256,768]{2,3,1,0:T(8,128)(2,1)} %copy.149), channel_id=1, source_target_pairs={{3,0},{0,1},{1,2},{2,3},{7,4},{4,5},{5,6},{6,7},{11,8},{8,9},{9,10... | collective-permute-start | bytes 2359304 | tf_op jit(solution)/shard_map/while/body/eval_jaxpr/ppermute | solution.py:19
  344.1 178.0 %collective-permute-start.6 = (bf16[2,1,256,768]{2,3,1,0:T(8,128)(2,1)}, bf16[2,1,256,768]{2,3,1,0:T(8,128)(2,1)}, u32[]{:S(2)}, u32[]{:S(2)}) collective-permute-start(bf16[2,1,256,768]{2,3,1,0:T(8,128)(2,1)} %fusion.114), channel_id=1, source_target_pairs={{3,0},{0,1},{1,2},{2,3},{7,4},{4,5},{5,6},{6,7},{11,8},{8,9},{9,10... | collective-permute-start | bytes 2359304 | tf_op jit(solution)/shard_map/ppermute | solution.py:19
  358.0 22.6 %collective-permute-start.5 = (bf16[2,1,256,768]{2,3,1,0:T(8,128)(2,1)}, bf16[2,1,256,768]{2,3,1,0:T(8,128)(2,1)}, u32[]{:S(2)}, u32[]{:S(2)}) collective-permute-start(bf16[2,1,256,768]{2,3,1,0:T(8,128)(2,1)} %fusion.452), channel_id=1, source_target_pairs={{3,0},{0,1},{1,2},{2,3},{7,4},{4,5},{5,6},{6,7},{11,8},{8,9},{9,10... | collective-permute-start | bytes 2359304 | tf_op jit(solution)/shard_map/while/body/eval_jaxpr/ppermute | solution.py:19
  358.0 33.9 %collective-permute-start.4 = (bf16[2,1,256,768]{2,3,1,0:T(8,128)(2,1)S(1)}, bf16[2,1,256,768]{2,3,1,0:T(8,128)(2,1)}, u32[]{:S(2)}, u32[]{:S(2)}) collective-permute-start(bf16[2,1,256,768]{2,3,1,0:T(8,128)(2,1)S(1)} %copy.137), channel_id=1, source_target_pairs={{3,0},{0,1},{1,2},{2,3},{7,4},{4,5},{5,6},{6,7},{11,8},{8,9},{9,10... | collective-permute-start | bytes 2359304 | tf_op jit(solution)/shard_map/while/body/eval_jaxpr/ppermute | solution.py:19
  400.9 22.6 %collective-permute-start.5 = (bf16[2,1,256,768]{2,3,1,0:T(8,128)(2,1)}, bf16[2,1,256,768]{2,3,1,0:T(8,128)(2,1)}, u32[]{:S(2)}, u32[]{:S(2)}) collective-permute-start(bf16[2,1,256,768]{2,3,1,0:T(8,128)(2,1)} %fusion.452), channel_id=1, source_target_pairs={{3,0},{0,1},{1,2},{2,3},{7,4},{4,5},{5,6},{6,7},{11,8},{8,9},{9,10... | collective-permute-start | bytes 2359304 | tf_op jit(solution)/shard_map/while/body/eval_jaxpr/ppermute | solution.py:19
  400.9 33.0 %collective-permute-start.4 = (bf16[2,1,256,768]{2,3,1,0:T(8,128)(2,1)S(1)}, bf16[2,1,256,768]{2,3,1,0:T(8,128)(2,1)}, u32[]{:S(2)}, u32[]{:S(2)}) collective-permute-start(bf16[2,1,256,768]{2,3,1,0:T(8,128)(2,1)S(1)} %copy.137), channel_id=1, source_target_pairs={{3,0},{0,1},{1,2},{2,3},{7,4},{4,5},{5,6},{6,7},{11,8},{8,9},{9,10... | collective-permute-start | bytes 2359304 | tf_op jit(solution)/shard_map/while/body/eval_jaxpr/ppermute | solution.py:19
  442.8 22.6 %collective-permute-start.5 = (bf16[2,1,256,768]{2,3,1,0:T(8,128)(2,1)}, bf16[2,1,256,768]{2,3,1,0:T(8,128)(2,1)}, u32[]{:S(2)}, u32[]{:S(2)}) collective-permute-start(bf16[2,1,256,768]{2,3,1,0:T(8,128)(2,1)} %fusion.452), channel_id=1, source_target_pairs={{3,0},{0,1},{1,2},{2,3},{7,4},{4,5},{5,6},{6,7},{11,8},{8,9},{9,10... | collective-permute-start | bytes 2359304 | tf_op jit(solution)/shard_map/while/body/eval_jaxpr/ppermute | solution.py:19
  442.8 32.1 %collective-permute-start.4 = (bf16[2,1,256,768]{2,3,1,0:T(8,128)(2,1)S(1)}, bf16[2,1,256,768]{2,3,1,0:T(8,128)(2,1)}, u32[]{:S(2)}, u32[]{:S(2)}) collective-permute-start(bf16[2,1,256,768]{2,3,1,0:T(8,128)(2,1)S(1)} %copy.137), channel_id=1, source_target_pairs={{3,0},{0,1},{1,2},{2,3},{7,4},{4,5},{5,6},{6,7},{11,8},{8,9},{9,10... | collective-permute-start | bytes 2359304 | tf_op jit(solution)/shard_map/while/body/eval_jaxpr/ppermute | solution.py:19
  483.6 39.8 %collective-permute-start.7 = (bf16[2,1,256,768]{2,3,1,0:T(8,128)(2,1)}, bf16[2,1,256,768]{2,3,1,0:T(8,128)(2,1)}, u32[]{:S(2)}, u32[]{:S(2)}) collective-permute-start(bf16[2,1,256,768]{2,3,1,0:T(8,128)(2,1)} %fusion.115), channel_id=1, source_target_pairs={{3,0},{0,1},{1,2},{2,3},{7,4},{4,5},{5,6},{6,7},{11,8},{8,9},{9,10... | collective-permute-start | bytes 2359304 | tf_op jit(solution)/shard_map/ppermute | solution.py:19
  534.4 27.9 %copy-start.33 = (f32[256,768]{1,0:T(8,128)}, f32[256,768]{1,0:T(8,128)S(1)}, u32[]{:S(2)}) copy-start(f32[256,768]{1,0:T(8,128)S(1)} %get-tuple-element.1491) | copy-start | bytes 2359300
  534.5 20.0 %copy-start.103 = (f32[768]{0:T(1024)S(1)}, f32[768]{0:T(1024)}, u32[]{:S(2)}) copy-start(f32[768]{0:T(1024)} %copy-done.102) | copy-start | bytes 9220
  565.7 51.0 %copy-start.112 = (f32[256]{0:T(256)S(1)}, f32[256]{0:T(256)}, u32[]{:S(2)}) copy-start(f32[256]{0:T(256)} %copy-done.110) | copy-start | bytes 3076
  565.8 52.6 %copy-start.32 = (f32[1,256,768]{2,1,0:T(8,128)S(1)}, f32[1,256,768]{2,1,0:T(8,128)}, u32[]{:S(2)}) copy-start(f32[1,256,768]{2,1,0:T(8,128)} %get-tuple-element.1392) | copy-start | bytes 2359300
  (182 other events, 797.4 us)
Sparse Core Ops, SparseCore 0:
  565.9 464.4 all-reduce.3
where the time goes:
time: 1070 us; the launch traced here: 1060 us
  waiting for transfers between devices  662 us (62%)
  matrix products  149 us (14%)
  local copies, waits for them, and re-layouts  95.2 us (9%)
  other arithmetic  92.4 us (9%)
  blocking collectives  42.2 us (4%)
  between operations  16.4 us (2%)
    psum x1, waiting for transfers between devices, local(): lax.psum((summed[0], summed[1], summed[2], summed[3], summed[4], summed[5...  410 us
    ppermute x20, waiting for transfers between devices, shifted(): return lax.ppermute(block, axis, route)  251 us
    unnamed x314, local copies, waits for them, and re-layouts  53.2 us
    psum x1, blocking collectives, local(): lax.psum((summed[0], summed[1], summed[2], summed[3], summed[4], summed[5...  42.2 us
  transfers between devices with their start and end apart: 21, of which 19 were waited for; matrix products, arithmetic and copies ran while one was open for 14% of the time, Pallas kernels for 0%

commit v1 on v0

--- a/solution.py
+++ b/solution.py
@@ -354,19 +354,22 @@
         )
     summed = functools.reduce(add_trees, collected)
     finals = lax.psum(
-        (
-            summed[0],
-            summed[1],
-            summed[2],
-            summed[3],
-            summed[4],
-            summed[5],
-            summed[6],
-            summed[7],
-            summed[8],
-            summed[9],
+        lax.psum(
+            (
+                summed[0],
+                summed[1],
+                summed[2],
+                summed[3],
+                summed[4],
+                summed[5],
+                summed[6],
+                summed[7],
+                summed[8],
+                summed[9],
+            ),
+            "narrow",
         ),
-        ("wide", "narrow"),
+        "wide",
     )
     return (
         jnp.concatenate(outputs, axis=0),

time: 1070 us -> 2000 us (1.87)
  waiting for transfers between devices: 662 us -> 1590 us
    psum x1, waiting for transfers between devices: 410 us -> 1020 us  [local(): lax.psum((summed[0], summed[1], summed[2], summed[3], summed[4], summed[5...]
    psum x0 -> x1, waiting for transfers between devices: none -> 319 us  [local(): lax.psum(lax.psum((summed[0], summed[1], summed[2], summed[3], summed[4],...]
    psum x0 -> x1, blocking collectives: none -> 25.6 us  [local(): lax.psum(lax.psum((summed[0], summed[1], summed[2], summed[3], summed[4],...]
    psum x1, blocking collectives: 42.2 us -> 17.8 us  [local(): lax.psum((summed[0], summed[1], summed[2], summed[3], summed[4], summed[5...]
    unnamed x314 -> x316, local copies, waits for them, and re-layouts: 53.2 us -> 51.8 us
  transfers between devices with their start and end apart: 21 -> 22, of which waited for: 19 -> 20; matrix products, arithmetic and copies ran while one was open for 14% -> 7% of each run, Pallas kernels for 0% -> 0%
where the time goes in v1:
time: 2000 us; the launch traced here: 1990 us
  waiting for transfers between devices  1590 us (80%)
  matrix products  149 us (7%)
  local copies, waits for them, and re-layouts  93.1 us (5%)
  other arithmetic  92.4 us (5%)
  blocking collectives  43.4 us (2%)
    psum x1, waiting for transfers between devices, local(): lax.psum((summed[0], summed[1], summed[2], summed[3], summed[4], summed[5...  1020 us
    psum x1, waiting for transfers between devices, local(): lax.psum(lax.psum((summed[0], summed[1], summed[2], summed[3], summed[4],...  319 us
    ppermute x20, waiting for transfers between devices, shifted(): return lax.ppermute(block, axis, route)  251 us
    unnamed x316, local copies, waits for them, and re-layouts  51.8 us
  transfers between devices with their start and end apart: 22, of which 20 were waited for; matrix products, arithmetic and copies ran while one was open for 7% of the time, Pallas kernels for 0%

profile of v1, /device:TPU:0, one launch (start us, length us, event | category | flops | bytes accessed | tf_op | source)
XLA Modules:
  0.0 1985.0 jit_solution(13095081780040925473)
XLA Ops:
  13.5 5.8 copy.51
  38.2 66.4 %while.85 = (s32[]{:T(128)}, bf16[2,1,256,768]{2,3,1,0:T(8,128)(2,1)}, f32[1,12,256]{2,1,0:T(8,128)}, f32[1,12,256]{2,1,0:T(8,128)}, f32[1,256,12,64]{1,3,2,0:T(...) while((s32[]{:T(128)}, ...), condition=%wide.region_15.16_spmd.clone, body=%wide.region_12.15_spmd.clone.sunk | while | flops 210586640 | bytes 25119744 | solution.py:195
  47.2 14.8 collective-permute-done.1
  68.0 15.7 collective-permute-done.1
  89.8 14.8 collective-permute-done.1
  106.7 57.2 %while.84 = (s32[]{:T(128)}, bf16[2,1,256,768]{2,3,1,0:T(8,128)(2,1)}, f32[1,12,256]{2,1,0:T(8,128)S(1)}, f32[1,12,256]{2,1,0:T(8,128)}, f32[1,256,12,64]{1,3,2,...) while((s32[]{:T(128)}, ...), condition=%wide.region_5.6_spmd.clone, body=%wide.region_2.5_spmd.clone.sunk | while | flops 210586640 | bytes 25070564 | solution.py:195
  112.1 14.5 collective-permute-done
  132.1 13.6 collective-permute-done
  151.0 12.7 collective-permute-done
  201.3 131.9 %while.86 = (s32[]{:T(128)}, bf16[2,1,256,768]{2,3,1,0:T(8,128)(2,1)}, f32[2,1,256,768]{2,3,1,0:T(8,128)}, f32[1,256,12,64]{1,3,2,0:T(8,128)}, s32[]{:T(128)}, /...) while((s32[]{:T(128)}, ...), condition=%wide.region_23.24_spmd.clone, body=%wide.region_22.23_spmd.clone.sunk | while | flops 513934336 | bytes 45259516 | solution.py:306
  215.6 20.1 %collective-permute-done.3 = bf16[2,1,256,768]{2,3,1,0:T(8,128)(2,1)} collective-permute-done((bf16[2,1,256,768]{2,3,1,0:T(8,128)(2,1)}, bf16[2,1,256,768]{2,3,1,0:T(8,128)(2,1)}, u32[]{:S(2)}, u32[]{:S(2)}) %collective-permute-start.3) | collective-permute-done | bytes 786464 | tf_op jit(solution)/shard_map/while/body/eval_jaxpr/ppermute | solution.py:19
  238.0 8.1 collective-permute-done.2
  260.7 19.8 collective-permute-done.3
  282.9 7.2 collective-permute-done.2
  304.7 19.8 collective-permute-done.3
  326.9 6.3 collective-permute-done.2
  346.9 125.6 %while.87 = (s32[]{:T(128)}, bf16[2,1,256,768]{2,3,1,0:T(8,128)(2,1)}, f32[2,1,256,768]{2,3,1,0:T(8,128)}, f32[1,256,12,64]{1,3,2,0:T(8,128)}, s32[]{:T(128)}, /...) while((s32[]{:T(128)}, ...), condition=%wide.region_29.30_spmd.clone, body=%wide.region_28.29_spmd.clone.sunk | while | flops 513934336 | bytes 42212092 | solution.py:306
  358.0 20.6 %collective-permute-done.5 = bf16[2,1,256,768]{2,3,1,0:T(8,128)(2,1)} collective-permute-done((bf16[2,1,256,768]{2,3,1,0:T(8,128)(2,1)}, bf16[2,1,256,768]{2,3,1,0:T(8,128)(2,1)}, u32[]{:S(2)}, u32[]{:S(2)}) %collective-permute-start.5) | collective-permute-done | bytes 786464 | tf_op jit(solution)/shard_map/while/body/eval_jaxpr/ppermute | solution.py:19
  381.0 8.8 collective-permute-done.4
  401.4 19.9 %collective-permute-done.5 = bf16[2,1,256,768]{2,3,1,0:T(8,128)(2,1)} collective-permute-done((bf16[2,1,256,768]{2,3,1,0:T(8,128)(2,1)}, bf16[2,1,256,768]{2,3,1,0:T(8,128)(2,1)}, u32[]{:S(2)}, u32[]{:S(2)}) %collective-permute-start.5) | collective-permute-done | bytes 786464 | tf_op jit(solution)/shard_map/while/body/eval_jaxpr/ppermute | solution.py:19
  423.7 7.9 collective-permute-done.4
  443.3 19.9 %collective-permute-done.5 = bf16[2,1,256,768]{2,3,1,0:T(8,128)(2,1)} collective-permute-done((bf16[2,1,256,768]{2,3,1,0:T(8,128)(2,1)}, bf16[2,1,256,768]{2,3,1,0:T(8,128)(2,1)}, u32[]{:S(2)}, u32[]{:S(2)}) %collective-permute-start.5) | collective-permute-done | bytes 786464 | tf_op jit(solution)/shard_map/while/body/eval_jaxpr/ppermute | solution.py:19
  465.6 6.9 collective-permute-done.4
  503.1 6.9 convolution_add_fusion.2
  510.1 6.3 convert_reduce_fusion.4
  552.0 7.9 convolution_add_fusion
  563.4 1015.1 %all-reduce.9.cloned.1.call-done = (f32[4608,128]{1,0:T(8,128)}, f32[768,2304]{1,0:T(8,128)}, f32[768,768]{1,0:T(8,128)}, f32[768,3072]{1,0:T(8,128)}, f32[3072,768]{1,0:T(8,128)}) async-done(((f32[4608,128]{1,0:T(8,128)}, f32[768,2304]{1,0:T(8,128)}, f32[768,768]{1,0:T(8,128)}, f32[768,3072]{1,0:T(8,128)}, f32[3072,768]{1,0:T(8,128)}), (f32[4608,128]{1,0:T(8,128)}, f32[768,2304]{1,0:T(8,128)}, ...) | async-done | bytes 30670864 | tf_op jit(solution)/shard_map/psum | solution.py:357
  1585.9 17.8 all-reduce.2
  1603.7 25.6 %all-reduce = (f32[4608]{0:T(1024)}, f32[768]{0:T(1024)}, f32[768]{0:T(1024)}, f32[3072]{0:T(1024)}, f32[768]{0:T(1024)}) all-reduce(f32[4608]{0:T(1024)S(1)} %get-tuple-element.1387, f32[768]{0:T(1024)S(1)} %get-tuple-element.1388, f32[768]{0:T(1024)S(1)} %get-tuple-element.1389, ...), channel_id=1, replica_groups=mesh['wide'=8,'narrow'=4] {'wide'}, use_global_device_ids=true, to_apply=%region_47.48 | all-reduce | flops 9984 | bytes 79872 | tf_op jit(solution)/shard_map/psum | solution.py:356
  1634.3 319.2 %all-reduce.7.cloned.1.call-done = (f32[4608,128]{1,0:T(8,128)}, f32[768,2304]{1,0:T(8,128)}, f32[768,768]{1,0:T(8,128)}, f32[768,3072]{1,0:T(8,128)}, f32[3072,768]{1,0:T(8,128)}) async-done(((f32[4608,128]{1,0:T(8,128)}, f32[768,2304]{1,0:T(8,128)}, f32[768,768]{1,0:T(8,128)}, f32[768,3072]{1,0:T(8,128)}, f32[3072,768]{1,0:T(8,128)}), (f32[4608,128]{1,0:T(8,128)}, f32[768,2304]{1,0:T(8,128)}, ...) | async-done | bytes 30670864 | tf_op jit(solution)/shard_map/psum | solution.py:356
  1956.7 6.6 copy.177
  1964.7 9.3 copy.179
  (691 shorter events, 295.3 us)
Async XLA Ops:
  7.2 166.9 %copy-start = (bf16[768,768]{1,0:T(8,128)(2,1)S(1)}, bf16[768,768]{1,0:T(8,128)(2,1)}, u32[]{:S(2)}) copy-start(bf16[768,768]{1,0:T(8,128)(2,1)} %param.31) | copy-start | bytes 3538948
  7.2 1571.3 %all-reduce.9.cloned.1.call-start = ((), (), s32[]{:S(2)}) async-start(), calls=%async_computation.1 | async-start | bytes 61341696 | tf_op jit(solution)/shard_map/psum | solution.py:357
  31.9 74.8 %copy-start.47 = (bf16[1,256,12,32]{1,3,2,0:T(8,128)(2,1)}, bf16[1,256,12,32]{1,3,2,0:T(8,128)(2,1)S(1)}, u32[]{:S(2)}) copy-start(bf16[1,256,12,32]{1,3,2,0:T(8,128)(2,1)S(1)} %get-tuple-element.1433) | copy-start | bytes 589828
  31.9 74.8 %copy-start.49 = (bf16[1,256,12,32]{1,3,2,0:T(8,128)(2,1)}, bf16[1,256,12,32]{1,3,2,0:T(8,128)(2,1)S(1)}, u32[]{:S(2)}) copy-start(bf16[1,256,12,32]{1,3,2,0:T(8,128)(2,1)S(1)} %get-tuple-element.1434) | copy-start | bytes 589828
  39.3 22.7 %collective-permute-start.1 = (bf16[2,1,256,768]{2,3,1,0:T(8,128)(2,1)S(1)}, bf16[2,1,256,768]{2,3,1,0:T(8,128)(2,1)}, u32[]{:S(2)}, u32[]{:S(2)}) collective-permute-start(bf16[2,1,256,768]{2,3,1,0:T(8,128)(2,1)S(1)} %copy.108), channel_id=1, source_target_pairs={{3,0},{0,1},{1,2},{2,3},{7,4},{4,5},{5,6},{6,7},{11,8},{8,9},{9,10... | collective-permute-start | bytes 2359304 | tf_op jit(solution)/shard_map/while/body/eval_jaxpr/ppermute | solution.py:19
  63.2 20.6 %collective-permute-start.1 = (bf16[2,1,256,768]{2,3,1,0:T(8,128)(2,1)S(1)}, bf16[2,1,256,768]{2,3,1,0:T(8,128)(2,1)}, u32[]{:S(2)}, u32[]{:S(2)}) collective-permute-start(bf16[2,1,256,768]{2,3,1,0:T(8,128)(2,1)S(1)} %copy.108), channel_id=1, source_target_pairs={{3,0},{0,1},{1,2},{2,3},{7,4},{4,5},{5,6},{6,7},{11,8},{8,9},{9,10... | collective-permute-start | bytes 2359304 | tf_op jit(solution)/shard_map/while/body/eval_jaxpr/ppermute | solution.py:19
  84.9 19.7 collective-permute-start.1
  107.9 18.8 collective-permute-start
  127.8 17.9 collective-permute-start
  146.8 16.9 collective-permute-start
  177.5 18.8 copy-start.23
  177.5 18.8 copy-start.119
  178.1 18.3 copy-start.135
  213.0 22.6 %collective-permute-start.3 = (bf16[2,1,256,768]{2,3,1,0:T(8,128)(2,1)}, bf16[2,1,256,768]{2,3,1,0:T(8,128)(2,1)}, u32[]{:S(2)}, u32[]{:S(2)}) collective-permute-start(bf16[2,1,256,768]{2,3,1,0:T(8,128)(2,1)} %fusion.436), channel_id=1, source_target_pairs={{3,0},{0,1},{1,2},{2,3},{7,4},{4,5},{5,6},{6,7},{11,8},{8,9},{9,10... | collective-permute-start | bytes 2359304 | tf_op jit(solution)/shard_map/while/body/eval_jaxpr/ppermute | solution.py:19
  213.0 33.1 %collective-permute-start.2 = (bf16[2,1,256,768]{2,3,1,0:T(8,128)(2,1)}, bf16[2,1,256,768]{2,3,1,0:T(8,128)(2,1)}, u32[]{:S(2)}, u32[]{:S(2)}) collective-permute-start(bf16[2,1,256,768]{2,3,1,0:T(8,128)(2,1)} %copy.149), channel_id=1, source_target_pairs={{3,0},{0,1},{1,2},{2,3},{7,4},{4,5},{5,6},{6,7},{11,8},{8,9},{9,10... | collective-permute-start | bytes 2359304 | tf_op jit(solution)/shard_map/while/body/eval_jaxpr/ppermute | solution.py:19
  257.9 22.6 %collective-permute-start.3 = (bf16[2,1,256,768]{2,3,1,0:T(8,128)(2,1)}, bf16[2,1,256,768]{2,3,1,0:T(8,128)(2,1)}, u32[]{:S(2)}, u32[]{:S(2)}) collective-permute-start(bf16[2,1,256,768]{2,3,1,0:T(8,128)(2,1)} %fusion.436), channel_id=1, source_target_pairs={{3,0},{0,1},{1,2},{2,3},{7,4},{4,5},{5,6},{6,7},{11,8},{8,9},{9,10... | collective-permute-start | bytes 2359304 | tf_op jit(solution)/shard_map/while/body/eval_jaxpr/ppermute | solution.py:19
  257.9 32.2 %collective-permute-start.2 = (bf16[2,1,256,768]{2,3,1,0:T(8,128)(2,1)}, bf16[2,1,256,768]{2,3,1,0:T(8,128)(2,1)}, u32[]{:S(2)}, u32[]{:S(2)}) collective-permute-start(bf16[2,1,256,768]{2,3,1,0:T(8,128)(2,1)} %copy.149), channel_id=1, source_target_pairs={{3,0},{0,1},{1,2},{2,3},{7,4},{4,5},{5,6},{6,7},{11,8},{8,9},{9,10... | collective-permute-start | bytes 2359304 | tf_op jit(solution)/shard_map/while/body/eval_jaxpr/ppermute | solution.py:19
  301.9 22.6 %collective-permute-start.3 = (bf16[2,1,256,768]{2,3,1,0:T(8,128)(2,1)}, bf16[2,1,256,768]{2,3,1,0:T(8,128)(2,1)}, u32[]{:S(2)}, u32[]{:S(2)}) collective-permute-start(bf16[2,1,256,768]{2,3,1,0:T(8,128)(2,1)} %fusion.436), channel_id=1, source_target_pairs={{3,0},{0,1},{1,2},{2,3},{7,4},{4,5},{5,6},{6,7},{11,8},{8,9},{9,10... | collective-permute-start | bytes 2359304 | tf_op jit(solution)/shard_map/while/body/eval_jaxpr/ppermute | solution.py:19
  301.9 31.2 %collective-permute-start.2 = (bf16[2,1,256,768]{2,3,1,0:T(8,128)(2,1)}, bf16[2,1,256,768]{2,3,1,0:T(8,128)(2,1)}, u32[]{:S(2)}, u32[]{:S(2)}) collective-permute-start(bf16[2,1,256,768]{2,3,1,0:T(8,128)(2,1)} %copy.149), channel_id=1, source_target_pairs={{3,0},{0,1},{1,2},{2,3},{7,4},{4,5},{5,6},{6,7},{11,8},{8,9},{9,10... | collective-permute-start | bytes 2359304 | tf_op jit(solution)/shard_map/while/body/eval_jaxpr/ppermute | solution.py:19
  342.0 177.7 %collective-permute-start.6 = (bf16[2,1,256,768]{2,3,1,0:T(8,128)(2,1)}, bf16[2,1,256,768]{2,3,1,0:T(8,128)(2,1)}, u32[]{:S(2)}, u32[]{:S(2)}) collective-permute-start(bf16[2,1,256,768]{2,3,1,0:T(8,128)(2,1)} %fusion.114), channel_id=1, source_target_pairs={{3,0},{0,1},{1,2},{2,3},{7,4},{4,5},{5,6},{6,7},{11,8},{8,9},{9,10... | collective-permute-start | bytes 2359304 | tf_op jit(solution)/shard_map/ppermute | solution.py:19
  356.0 22.6 %collective-permute-start.5 = (bf16[2,1,256,768]{2,3,1,0:T(8,128)(2,1)}, bf16[2,1,256,768]{2,3,1,0:T(8,128)(2,1)}, u32[]{:S(2)}, u32[]{:S(2)}) collective-permute-start(bf16[2,1,256,768]{2,3,1,0:T(8,128)(2,1)} %fusion.452), channel_id=1, source_target_pairs={{3,0},{0,1},{1,2},{2,3},{7,4},{4,5},{5,6},{6,7},{11,8},{8,9},{9,10... | collective-permute-start | bytes 2359304 | tf_op jit(solution)/shard_map/while/body/eval_jaxpr/ppermute | solution.py:19
  356.0 33.8 %collective-permute-start.4 = (bf16[2,1,256,768]{2,3,1,0:T(8,128)(2,1)S(1)}, bf16[2,1,256,768]{2,3,1,0:T(8,128)(2,1)}, u32[]{:S(2)}, u32[]{:S(2)}) collective-permute-start(bf16[2,1,256,768]{2,3,1,0:T(8,128)(2,1)S(1)} %copy.137), channel_id=1, source_target_pairs={{3,0},{0,1},{1,2},{2,3},{7,4},{4,5},{5,6},{6,7},{11,8},{8,9},{9,10... | collective-permute-start | bytes 2359304 | tf_op jit(solution)/shard_map/while/body/eval_jaxpr/ppermute | solution.py:19
  398.7 22.6 %collective-permute-start.5 = (bf16[2,1,256,768]{2,3,1,0:T(8,128)(2,1)}, bf16[2,1,256,768]{2,3,1,0:T(8,128)(2,1)}, u32[]{:S(2)}, u32[]{:S(2)}) collective-permute-start(bf16[2,1,256,768]{2,3,1,0:T(8,128)(2,1)} %fusion.452), channel_id=1, source_target_pairs={{3,0},{0,1},{1,2},{2,3},{7,4},{4,5},{5,6},{6,7},{11,8},{8,9},{9,10... | collective-permute-start | bytes 2359304 | tf_op jit(solution)/shard_map/while/body/eval_jaxpr/ppermute | solution.py:19
  398.8 32.9 %collective-permute-start.4 = (bf16[2,1,256,768]{2,3,1,0:T(8,128)(2,1)S(1)}, bf16[2,1,256,768]{2,3,1,0:T(8,128)(2,1)}, u32[]{:S(2)}, u32[]{:S(2)}) collective-permute-start(bf16[2,1,256,768]{2,3,1,0:T(8,128)(2,1)S(1)} %copy.137), channel_id=1, source_target_pairs={{3,0},{0,1},{1,2},{2,3},{7,4},{4,5},{5,6},{6,7},{11,8},{8,9},{9,10... | collective-permute-start | bytes 2359304 | tf_op jit(solution)/shard_map/while/body/eval_jaxpr/ppermute | solution.py:19
  440.6 22.6 %collective-permute-start.5 = (bf16[2,1,256,768]{2,3,1,0:T(8,128)(2,1)}, bf16[2,1,256,768]{2,3,1,0:T(8,128)(2,1)}, u32[]{:S(2)}, u32[]{:S(2)}) collective-permute-start(bf16[2,1,256,768]{2,3,1,0:T(8,128)(2,1)} %fusion.452), channel_id=1, source_target_pairs={{3,0},{0,1},{1,2},{2,3},{7,4},{4,5},{5,6},{6,7},{11,8},{8,9},{9,10... | collective-permute-start | bytes 2359304 | tf_op jit(solution)/shard_map/while/body/eval_jaxpr/ppermute | solution.py:19
  440.6 31.9 %collective-permute-start.4 = (bf16[2,1,256,768]{2,3,1,0:T(8,128)(2,1)S(1)}, bf16[2,1,256,768]{2,3,1,0:T(8,128)(2,1)}, u32[]{:S(2)}, u32[]{:S(2)}) collective-permute-start(bf16[2,1,256,768]{2,3,1,0:T(8,128)(2,1)S(1)} %copy.137), channel_id=1, source_target_pairs={{3,0},{0,1},{1,2},{2,3},{7,4},{4,5},{5,6},{6,7},{11,8},{8,9},{9,10... | collective-permute-start | bytes 2359304 | tf_op jit(solution)/shard_map/while/body/eval_jaxpr/ppermute | solution.py:19
  481.4 39.7 %collective-permute-start.7 = (bf16[2,1,256,768]{2,3,1,0:T(8,128)(2,1)}, bf16[2,1,256,768]{2,3,1,0:T(8,128)(2,1)}, u32[]{:S(2)}, u32[]{:S(2)}) collective-permute-start(bf16[2,1,256,768]{2,3,1,0:T(8,128)(2,1)} %fusion.115), channel_id=1, source_target_pairs={{3,0},{0,1},{1,2},{2,3},{7,4},{4,5},{5,6},{6,7},{11,8},{8,9},{9,10... | collective-permute-start | bytes 2359304 | tf_op jit(solution)/shard_map/ppermute | solution.py:19
  532.1 27.9 %copy-start.33 = (f32[256,768]{1,0:T(8,128)}, f32[256,768]{1,0:T(8,128)S(1)}, u32[]{:S(2)}) copy-start(f32[256,768]{1,0:T(8,128)S(1)} %get-tuple-element.1501) | copy-start | bytes 2359300
  532.1 19.9 %copy-start.104 = (f32[768]{0:T(1024)S(1)}, f32[768]{0:T(1024)}, u32[]{:S(2)}) copy-start(f32[768]{0:T(1024)} %copy-done.103) | copy-start | bytes 9220
  563.3 1390.2 %all-reduce.7.cloned.1.call-start = ((), (), s32[]{:S(2)}) async-start(), calls=%async_computation | async-start | bytes 61341696 | tf_op jit(solution)/shard_map/psum | solution.py:356
  1578.5 52.2 %copy-start.113 = (f32[256]{0:T(256)S(1)}, f32[256]{0:T(256)}, u32[]{:S(2)}) copy-start(f32[256]{0:T(256)} %copy-done.111) | copy-start | bytes 3076
  1578.5 53.7 %copy-start.32 = (f32[1,256,768]{2,1,0:T(8,128)S(1)}, f32[1,256,768]{2,1,0:T(8,128)}, u32[]{:S(2)}) copy-start(f32[1,256,768]{2,1,0:T(8,128)} %get-tuple-element.1402) | copy-start | bytes 2359300
  (184 other events, 834.2 us)
Sparse Core Ops, SparseCore 0:
  563.4 1014.9 all-reduce.8
  1583.9 369.5 all-reduce.6
